TPU v7x, 256 devices: a whole 4x4x8 slice. The times are simulated.
256 devices in a mesh: seq: 32 (over z, y_hi, core), tp: 8 (over y_lo, x).
Axes of the slice: x: 4, y: 4 (y_hi: 2, y_lo: 2; y = y_hi * 2 + y_lo), z: 8, core: 2. Of those that a mesh axis runs over, the one named last changes fastest.
Arguments:
- queries: bfloat16 [8192, 5120], P('seq', 'tp'), may hold values from -120 to 120, as said below
- prompt_keys: bfloat16 [4096, 1024], P('seq', 'tp'), may hold values from -4 to 4
- prompt_values: bfloat16 [4096, 1024], P('seq', 'tp'), may hold values from -6 to 6
- response_keys: bfloat16 [8192, 1024], P('seq', 'tp'), may hold values from -6 to 6
- response_values: bfloat16 [8192, 1024], P('seq', 'tp'), may hold values from -6 to 6
- lengths: int32 [16], replicated, may hold values from 1 to 4096, 8192 in all
- out_weight: bfloat16 [5120, 5120], P('tp'), may hold values from -0.125 to 0.125
Outputs:
- projected: bfloat16 [8192, 5120], P('seq', 'tp')
Inputs may be any that keep to these rules, and one draw needn't show every extreme that they name: `queries`: in a few rows a query head may be a multiple of a prompt key of its key head. 16 lengths that sum to 8192; the longest has exactly 4096 tokens.
All inputs are finite; a program needn't handle non-finite values.
Results may differ from a plain program's by a relative error of at most 0.014.
Values may be sent and summed in bfloat16 or wider, within the bound.
A program may use at most 192 MiB of HBM per device.

v0:
```python
import jax
import jax.numpy as jnp
from jax import lax
from jax.sharding import PartitionSpec as P

HEADS = 40
KVH = 8
HD = 128


def segment_layout(lengths, first_row, row_count):
    positions = first_row + jnp.arange(row_count, dtype=jnp.int32)
    seg_ends = jnp.cumsum(lengths)
    seg_starts = seg_ends - lengths
    inside = (positions[:, None] >= seg_starts[None, :]) & (positions[:, None] < seg_ends[None, :])
    own_start = jnp.sum(jnp.where(inside, seg_starts[None, :], 0), axis=1)
    return (positions, own_start)


def update_state(running, grouped, key_block, value_block, visible, scale_factor):
    maximum, summed, weighted = running
    scores = (
        jnp.einsum("rkgd,nkd->rkgn", grouped, key_block, preferred_element_type=jnp.float32)
        * scale_factor
    )
    if visible is not None:
        scores = jnp.where(visible[:, None, None, :], scores, -jnp.inf)
    new_max = jnp.maximum(maximum, jnp.max(scores, axis=3))
    weights = jnp.exp(scores - new_max[..., None])
    rescale = jnp.exp(maximum - new_max)
    rounded = weights.astype(jnp.bfloat16)
    summed = summed * rescale + jnp.sum(weights, axis=3)
    weighted = weighted * rescale[..., None] + jnp.einsum(
        "rkgn,nkd->rkgd", rounded, value_block, preferred_element_type=jnp.float32
    )
    return (new_max, summed, weighted)


def per_device(
    queries, prompt_keys, prompt_values, response_keys, response_values, lengths, out_weight
):
    row_count = queries.shape[0]
    kv_local = prompt_keys.shape[1] // HD
    group_size = HEADS // KVH
    scale_factor = HD ** (-0.5)
    grouped = queries.reshape(row_count, kv_local, group_size, HD)
    first_row = lax.axis_index("seq") * row_count
    positions, own_start = segment_layout(lengths, first_row, row_count)
    softmax_state = (
        jnp.full((row_count, kv_local, group_size), -jnp.inf, jnp.float32),
        jnp.zeros((row_count, kv_local, group_size), jnp.float32),
        jnp.zeros((row_count, kv_local, group_size, HD), jnp.float32),
    )
    prompt_pair = jnp.stack([prompt_keys, prompt_values])
    fragment = lax.all_gather(prompt_pair, "seq", axis=1, tiled=True)
    frag_rows = fragment.shape[1]
    key_block = fragment[0].reshape(frag_rows, kv_local, HD)
    value_block = fragment[1].reshape(frag_rows, kv_local, HD)
    softmax_state = update_state(softmax_state, grouped, key_block, value_block, None, scale_factor)
    response_pair = jnp.stack([response_keys, response_values])
    fragment = lax.all_gather(response_pair, "seq", axis=1, tiled=True)
    frag_rows = fragment.shape[1]
    key_pos = jnp.arange(frag_rows, dtype=jnp.int32)
    visible = (key_pos[None, :] <= positions[:, None]) & (key_pos[None, :] >= own_start[:, None])
    key_block = fragment[0].reshape(frag_rows, kv_local, HD)
    value_block = fragment[1].reshape(frag_rows, kv_local, HD)
    softmax_state = update_state(
        softmax_state, grouped, key_block, value_block, visible, scale_factor
    )
    maximum, summed, weighted = softmax_state
    attended = (
        (weighted / summed[..., None])
        .astype(jnp.bfloat16)
        .reshape(row_count, kv_local * group_size * HD)
    )
    partial_out = jnp.dot(attended, out_weight, preferred_element_type=jnp.float32)
    return lax.psum_scatter(partial_out.astype(jnp.bfloat16), "tp", scatter_dimension=1, tiled=True)


def solution(mesh):
    in_specs = (
        P("seq", "tp"),
        P("seq", "tp"),
        P("seq", "tp"),
        P("seq", "tp"),
        P("seq", "tp"),
        P(),
        P("tp", None),
    )
    out_specs = P("seq", "tp")
    return jax.shard_map(
        per_device, mesh=mesh, in_specs=in_specs, out_specs=out_specs, check_vma=False
    )
```

profile of v0, /device:TPU:8, one launch (start us, length us, event | category | flops | bytes accessed | tf_op | source)
XLA Modules:
  0.0 299.2 jit_solution(3897833121249140386)
XLA Ops:
  6.5 0.0 all-gather.3.cloned.1.call-start
  6.5 1.4 pad_maximum_fusion.1
  7.9 0.0 all-gather.3.cloned.1.call-update
  8.0 0.0 all-gather.5.cloned.1.call-start
  8.0 1.5 pad_maximum_fusion
  9.6 0.0 all-gather.5.cloned.1.call-update
  9.6 0.0 reduce-scatter.4.cloned.1.call-start
  9.6 0.7 copy.35
  10.4 0.1 reduce.4
  10.5 0.7 sub.50
  11.2 1.1 copy.31
  12.3 0.1 select_reduce_fusion
  12.4 2.0 fusion.13
  14.5 0.0 copy-start.2
  14.5 77.5 %all-gather.3.cloned.1.call-done = bf16[2,4096,128]{2,1,0:T(8,128)(2,1)} async-done(((bf16[2,128,128]{2,1,0:T(8,128)(2,1)}), bf16[2,4096,128]{2,1,0:T(8,128)(2,1)}) %all-gather.3.cloned.1.call-update) | async-done | bytes 2097168 | tf_op jit(solution)/shard_map/all_gather | solution.py:55
  91.9 4.1 %bitcast_reduce_fusion = (f32[256,5]{0,1:T(8,128)S(1)}, f32[4096,256,5]{1,0,2:T(8,128)S(1)}) fusion(bf16[256,5,128]{0,2,1:T(8,128)(2,1)S(1)} %bitcast.121, bf16[2,4096,128]{2,1,0:T(8,128)(2,1)} %all-gather.3.cloned.1.call-done), kind=kOutput, calls=%fused_computation.7 | convolution fusion | flops 1352661760 | bytes 22352896 | tf_op jit(solution)/shard_map/rkgd,nkd->rkgn/dot_general | solution.py:23
  96.0 0.0 copy-start
  96.1 7.0 %copy-done = f32[4096,256,5]{1,0,2:T(8,128)} copy-done((f32[4096,256,5]{1,0,2:T(8,128)}, f32[4096,256,5]{1,0,2:T(8,128)S(1)}, u32[]{:S(2)}) %copy-start) | copy-done | bytes 20971544
  103.0 3.8 %fusion.8 = f32[256,5]{0,1:T(8,128)S(1)} fusion(f32[4096,256,5]{1,0,2:T(8,128)S(1)} %get-tuple-element.9, f32[256,5]{0,1:T(8,128)S(1)} %get-tuple-element.8), kind=kLoop, calls=%fused_computation.11 | loop fusion | flops 15727360 | bytes 20981760 | tf_op jit(solution)/shard_map/reduce_sum | solution.py:32
  106.9 71.1 %all-gather.5.cloned.1.call-done = bf16[2,8192,128]{2,1,0:T(8,128)(2,1)} async-done(((bf16[2,256,128]{2,1,0:T(8,128)(2,1)}), bf16[2,8192,128]{2,1,0:T(8,128)(2,1)}) %all-gather.5.cloned.1.call-update) | async-done | bytes 4194320 | tf_op jit(solution)/shard_map/all_gather | solution.py:61
  177.9 0.0 copy-done.2
  177.9 18.1 %fusion.2 = (f32[256,5]{0,1:T(8,128)S(1)}, f32[8192,256,5]{1,0,2:T(8,128)}) fusion(pred[256,8192]{0,1:T(8,128)(4,1)S(1)} %fusion.13, bf16[256,5,128]{0,2,1:T(8,128)(2,1)S(1)} %bitcast.122, bf16[2,8192,128]{2,1,0:T(8,128)(2,1)} %all-gather.5.cloned.1.call-done), kind=kOutput, calls=%fused_computation.4 | convolution fusion | flops 2715810560 | bytes 46470144 | tf_op jit(solution)/shard_map/rkgd,nkd->rkgn/dot_general | solution.py:23
  196.0 0.0 copy-start.1
  196.0 18.6 %fusion = f32[256,5]{0,1:T(8,128)S(1)} fusion(f32[8192,256,5]{1,0,2:T(8,128)} %get-tuple-element.11, f32[256,5]{0,1:T(8,128)S(1)} %max.17, pred[256,8192]{0,1:T(8,128)(4,1)} %copy-done.2), kind=kLoop, calls=%fused_computation.2 | loop fusion | flops 41941760 | bytes 44050432 | tf_op jit(solution)/shard_map/reduce_sum | solution.py:32
  214.7 1.1 copy-done.1
  215.8 4.5 %fusion.27 = f32[1,128,256,5]{2,1,3,0:T(8,128)S(1)} fusion(f32[4096,256,5]{1,0,2:T(8,128)S(1)} %copy-done.1, f32[256,5]{0,1:T(8,128)S(1)} %get-tuple-element.8, bf16[2,4096,128]{2,1,0:T(8,128)(2,1)} %all-gather.3.cloned.1.call-done, f32[256,5]{0,1:T(8,128)S(1)} %get-tuple-element.6, f32[256,5]{0,1:T(8,128)S(1)} %get-tuple-element.7), kind=kOutput, calls=%fused_computation.26 | convolution fusion | flops 1358233600 | bytes 22690816 | tf_op jit(solution)/shard_map/rkgn,nkd->rkgd/dot_general | solution.py:33
  220.2 18.8 %fusion.34 = bf16[1,128,256,5]{2,1,3,0:T(8,128)(2,1)S(1)} fusion(f32[1,128,256,5]{2,1,3,0:T(8,128)S(1)} %fusion.27, f32[8192,256,5]{1,0,2:T(8,128)} %get-tuple-element.11, f32[256,5]{0,1:T(8,128)S(1)} %max.17, pred[256,8192]{0,1:T(8,128)(4,1)} %copy-done.2, bf16[2,8192,128]{2,1,0:T(8,128)(2,1)} %all-gather.5.cloned.1.call-done, ...), kind=kOutput, calls=%fused_computation.31 | convolution fusion | flops 2726789120 | bytes 47130624 | tf_op jit(solution)/shard_map/rkgn,nkd->rkgd/dot_general | solution.py:33
  239.0 5.1 %convolution_convert_fusion = bf16[256,5120]{1,0:T(8,128)(2,1)S(1)} fusion(bf16[256,640]{0,1:T(8,128)(2,1)S(1)} %bitcast.123, bf16[640,5120]{1,0:T(8,128)(2,1)} %param.13), kind=kOutput, calls=%fused_computation.18 | convolution fusion | flops 1679032320 | bytes 9502720 | tf_op jit(solution)/shard_map/dot_general | solution.py:76
  244.1 2.6 copy.47
  246.7 0.0 reduce-scatter.4.cloned.1.call-update
  246.7 44.1 %reduce-scatter.4.cloned.1.call-done = bf16[640,256]{1,0:T(8,128)(2,1)} async-done(((bf16[5120,256]{1,0:T(8,128)(2,1)}), bf16[640,256]{1,0:T(8,128)(2,1)}) %reduce-scatter.4.cloned.1.call-update) | async-done | bytes 327696
  290.8 1.9 copy.48
  (4 shorter events, 0.1 us)
Async XLA Ops:
  6.5 85.4 %all-gather.3.cloned.1.call-start = ((), (), s32[]{:S(2)}) async-start(), calls=%async_computation.1 | async-start | bytes 2162688 | tf_op jit(solution)/shard_map/all_gather | solution.py:55
  8.0 170.0 %all-gather.5.cloned.1.call-start = ((), (), s32[]{:S(2)}) async-start(), calls=%async_computation.2 | async-start | bytes 4325376 | tf_op jit(solution)/shard_map/all_gather | solution.py:61
  9.6 281.3 %reduce-scatter.4.cloned.1.call-start = ((), (), s32[]{:S(2)}) async-start(), calls=%async_computation.3 | async-start | bytes 2949120
  14.5 163.5 %copy-start.2 = (pred[256,8192]{0,1:T(8,128)(4,1)}, pred[256,8192]{0,1:T(8,128)(4,1)S(1)}, u32[]{:S(2)}) copy-start(pred[256,8192]{0,1:T(8,128)(4,1)S(1)} %fusion.13) | copy-start | bytes 6291460
  96.0 7.0 %copy-start = (f32[4096,256,5]{1,0,2:T(8,128)}, f32[4096,256,5]{1,0,2:T(8,128)S(1)}, u32[]{:S(2)}) copy-start(f32[4096,256,5]{1,0,2:T(8,128)S(1)} %get-tuple-element.9) | copy-start | bytes 62914564
  196.0 19.7 %copy-start.1 = (f32[4096,256,5]{1,0,2:T(8,128)S(1)}, f32[4096,256,5]{1,0,2:T(8,128)}, u32[]{:S(2)}) copy-start(f32[4096,256,5]{1,0,2:T(8,128)} %copy-done) | copy-start | bytes 62914564
Sparse Core Ops, SparseCore 0:
  10.2 81.7 all-gather.2
  94.8 83.1 all-gather.4
  246.8 43.9 reduce-scatter.3
where the time goes:
time: 300 us; the launch traced here: 299 us
  waiting for transfers between devices  193 us (64%)
  matrix products  50.5 us (17%)
  other arithmetic  28.3 us (9%)
  local copies, waits for them, and re-layouts  14.4 us (5%)
  between operations  13.2 us (4%)
    all_gather x1, waiting for transfers between devices, per_device(): fragment = lax.all_gather(prompt_pair, 'seq', axis=1, tiled=True)  77.5 us
    all_gather x1, waiting for transfers between devices, per_device(): fragment = lax.all_gather(response_pair, 'seq', axis=1, tiled=True)  71.1 us
    unnamed x4, waiting for transfers between devices  44.2 us
    dot_general x2, matrix products, update_state(): jnp.einsum('rkgn,nkd->rkgd', rounded, value_block, preferred_element_type...  23.2 us
    reduce_sum x2, other arithmetic, update_state(): summed = summed * rescale + jnp.sum(weights, axis=3)  22.4 us
    dot_general x2, matrix products, update_state(): jnp.einsum('rkgd,nkd->rkgn', grouped, key_block, preferred_element_type=j...  22.2 us
    unnamed x9, local copies, waits for them, and re-layouts  13.6 us
  transfers between devices with their start and end apart: 3, of which 3 were waited for; matrix products, arithmetic and copies ran while one was open for 5% of the time, Pallas kernels for 0%

commit v1 on v0

v1 whole, which is shorter than its diff:
```python
import functools

import jax
import jax.numpy as jnp
from jax import lax
from jax.experimental import pallas as pl
from jax.experimental.pallas import tpu as pltpu
from jax.sharding import PartitionSpec as P

HEADS = 40
KVH = 8
HD = 128
GROUP = HEADS // KVH
N_RESP = 16
PLANES = 8
SLOTS = 32
PROWS = 128
RROWS = 256
SCALE = HD**-0.5 * 1.4426950408889634
LOW = -1e30
MESH = pl.DeviceIdType.MESH


PLAN = [
    ([(0, 1, 0), (0, -1, 0), (0, 0, 1)], 0, [(0, 0), (0, 2), (1, 0), (-1, 0), (0, 1), (1, 2), (-1, 2), (0, 3)], [[(0, 2, 0), (1, 1, 0)]]),
    ([(1, 0, 1), (0, 1, 1), (0, -2, 0), (0, -1, 1), (0, 3, 0)], 0, [(2, 0), (1, 1), (-2, 0), (2, 2), (-1, 1), (3, 0), (1, 3), (-2, 2)], [[(0, 2, 1)]]),
    ([(1, 1, 1), (1, 2, 0), (0, 4, 0)], 1, [(1, 0), (1, 2), (1, 1), (2, 0)], [[(0, -2, 1), (0, 3, 1)]]),
    ([(0, 5, 0)], 0, [(-1, 3), (3, 2), (2, 1), (2, 3), (4, 0), (-2, 1), (3, 1), (4, 2)], [[(1, 3, 0), (0, 4, 1)]]),
    ([(1, 2, 1)], 1, [(1, 3), (2, 2), (3, 0), (2, 1)], [[(0, 5, 1)]]),
    ([(1, 4, 0)], 0, [(-2, 3), (3, 3), (5, 0), (5, 2), (4, 1), (4, 3), (5, 1), (5, 3)], [[(1, 3, 1)]]),
    ([], 1, [(3, 2), (2, 3), (3, 1), (3, 3)], [[]]),
    ([(1, 4, 1)], 2, [(4, 0), (4, 1), (4, 2), (4, 3), (0, 0), (0, 1), (0, 2), (0, 3)], [[]]),
]

SPLIT = (2, 5)
DOWN, UP = 5, 2


def attend(q_ref, keys, values, bias_ref, top_ref, acc_ref, heads):
    count = keys.shape[0]
    widened = jnp.concatenate([values, jnp.ones((count, HD), jnp.bfloat16)], axis=1)
    for head in heads:
        scores = lax.dot_general(
            q_ref[:, head * HD : (head + 1) * HD],
            keys,
            (((1,), (1,)), ((), ())),
            preferred_element_type=jnp.float32,
        )
        if bias_ref is not None:
            scores = scores + bias_ref[:, :count]
        before = top_ref[head]
        top = jnp.maximum(before, jnp.max(scores, axis=1, keepdims=True) * SCALE)
        weights = jnp.exp2(scores * SCALE - top).astype(jnp.bfloat16)
        top_ref[head] = top
        acc_ref[head] = acc_ref[head] * jnp.exp2(before - top) + jnp.dot(
            weights, widened, preferred_element_type=jnp.float32
        )


def gather_attend(
    lengths_ref, q_ref, pk_ref, pv_ref, rk_ref, rv_ref, out_ref,
    pbuf, rbuf, top_ref, acc_ref, bias_ref, first_ref, load_sem, send_sem, recv_sem,
):
    s = lax.axis_index("seq")
    z, b = s // 4, s % 4
    h, c = b // 2, b % 2
    sibling = {"seq": z * 4 + h * 2 + (1 - c)}
    across = {"seq": z * 4 + (1 - h) * 2 + c}
    up = {"seq": ((z + 1) % PLANES) * 4 + b}
    down = {"seq": ((z + PLANES - 1) % PLANES) * 4 + b}
    order = [h * 2 + c, (1 - h) * 2 + c, h * 2 + (1 - c), (1 - h) * 2 + (1 - c)]

    loads = []
    for n, (src, dst) in enumerate(
        [(pk_ref, pbuf.at[s, 0]), (pv_ref, pbuf.at[s, 1]), (rk_ref, rbuf.at[s, 0]), (rv_ref, rbuf.at[s, 1])]
    ):
        loads.append(pltpu.make_async_copy(src, dst, load_sem.at[n]))
        loads[-1].start()

    barrier = pltpu.get_barrier_semaphore()
    for peer in (sibling, across, up, down):
        pl.semaphore_signal(barrier, inc=1, device_id=peer, device_id_type=MESH)

    def slot_of(kind, away, which):
        plane = (z + (PLANES - away if kind else PLANES + away)) % PLANES
        return plane * 4 + order[which]

    def copy(kind, slot, way, peer):
        buf = rbuf if kind else pbuf
        return pltpu.make_async_remote_copy(
            src_ref=buf.at[slot],
            dst_ref=buf.at[slot],
            send_sem=send_sem.at[kind, way, slot],
            recv_sem=recv_sem.at[kind, slot],
            device_id=peer,
            device_id_type=MESH,
        )

    sends = []

    def send(*what):
        sending = copy(*what)
        sending.start()
        sends.append(sending)

    def pass_on(kind, away, which):
        slot = slot_of(kind, away, which)
        if kind == 0:
            if away == 0 and which == 0:
                send(kind, slot, 2, across)
            if 0 <= away < DOWN:
                send(kind, slot, 1, down)
            if -UP < away <= 0:
                send(kind, slot, 3, up)
            send(kind, slot, 0, sibling)
        else:
            if which == 0:
                if away < 4:
                    send(kind, slot, 1, up)
                send(kind, slot, 2, across)
            send(kind, slot, 0, sibling)

    taken = {(0, 0, 0), (1, 0, 0)}

    def take(shard):
        if shard not in taken:
            taken.add(shard)
            copy(shard[0], slot_of(*shard), 0, sibling).wait_recv()
            if shard[2] < 2:
                pass_on(*shard)

    for copying in loads:
        copying.wait()
    pl.semaphore_wait(barrier, 4)
    pass_on(0, 0, 0)
    pass_on(1, 0, 0)

    position = s * RROWS + lax.broadcasted_iota(jnp.int32, (RROWS, 1), 0)
    first = jnp.zeros((RROWS, 1), jnp.int32)
    start = jnp.int32(0)
    for r in range(N_RESP):
        first = jnp.where(position >= start, start, first)
        start = start + lengths_ref[r]
    first_ref[...] = first
    top_ref[...] = jnp.full_like(top_ref, LOW)
    acc_ref[...] = jnp.zeros_like(acc_ref)

    def visible(slot, at):
        position = s * RROWS + lax.broadcasted_iota(jnp.int32, (RROWS, 1), 0)
        key = slot * RROWS + lax.broadcasted_iota(jnp.int32, (RROWS, RROWS), 1)
        seen = (key >= first_ref[...]) & (key <= position)
        bias_ref[:, at * RROWS : (at + 1) * RROWS] = jnp.where(seen, 0.0, LOW)

    for before, kind, shards, between in PLAN:
        for shard in before:
            take(shard)
        for away, which in shards:
            take((min(kind, 1), away, which))
        if kind < 2:
            chosen = [slot_of(kind, *shard) for shard in shards]
        else:
            chosen = []
            for i in range(5):
                own = jnp.where(i <= b, 1, 0)
                below = (z + PLANES - 4) % PLANES
                chosen.append(own * (4 * z + min(i, 3)) + (1 - own) * (4 * below + max(i - 1, 0)))
        buf = rbuf if kind else pbuf
        if kind:
            for n, slot in enumerate(chosen):
                visible(slot, n)
        keys, values = [jnp.concatenate([buf[slot, n] for slot in chosen], axis=0) for n in range(2)]
        edges = (0,) + SPLIT
        for n in range(len(SPLIT)):
            attend(q_ref, keys, values, bias_ref if kind else None, top_ref, acc_ref, range(edges[n], edges[n + 1]))
            if n < len(between):
                for shard in between[n]:
                    take(shard)

    for head in range(GROUP):
        acc = acc_ref[head]
        out_ref[:, head * HD : (head + 1) * HD] = (acc[:, :HD] / acc[:, HD:]).astype(jnp.bfloat16)

    for sending in sends:
        sending.wait_send()


def per_device(queries, prompt_keys, prompt_values, response_keys, response_values, lengths, out_weight):
    vmem = pl.BlockSpec(memory_space=pltpu.VMEM)
    attended = pl.pallas_call(
        gather_attend,
        out_shape=jax.ShapeDtypeStruct(queries.shape, jnp.bfloat16),
        in_specs=[pl.BlockSpec(memory_space=pltpu.SMEM), vmem] + [pl.BlockSpec(memory_space=pl.ANY)] * 4,
        out_specs=vmem,
        scratch_shapes=[
            pltpu.VMEM((SLOTS, 2, PROWS, HD), jnp.bfloat16),
            pltpu.VMEM((SLOTS, 2, RROWS, HD), jnp.bfloat16),
            pltpu.VMEM((GROUP, RROWS, 1), jnp.float32),
            pltpu.VMEM((GROUP, RROWS, 2 * HD), jnp.float32),
            pltpu.VMEM((RROWS, 5 * RROWS), jnp.float32),
            pltpu.VMEM((RROWS, 1), jnp.int32),
            pltpu.SemaphoreType.DMA((4,)),
            pltpu.SemaphoreType.DMA((2, 4, SLOTS)),
            pltpu.SemaphoreType.DMA((2, SLOTS)),
        ],
        compiler_params=pltpu.CompilerParams(
            collective_id=0, has_side_effects=True, vmem_limit_bytes=60 * 2**20
        ),
        name="gather_attend",
    )(lengths, queries, prompt_keys, prompt_values, response_keys, response_values)
    partial_out = jnp.dot(attended, out_weight, preferred_element_type=jnp.float32)
    return lax.psum_scatter(partial_out.astype(jnp.bfloat16), "tp", scatter_dimension=1, tiled=True)


def solution(mesh):
    in_specs = (P("seq", "tp"), P("seq", "tp"), P("seq", "tp"), P("seq", "tp"), P("seq", "tp"), P(), P("tp", None))
    return jax.shard_map(
        per_device, mesh=mesh, in_specs=in_specs, out_specs=P("seq", "tp"), check_vma=False
    )
```

time: 300 us -> 113 us (0.38)
  waiting for transfers between devices: 193 us -> 45.4 us
  matrix products: 50.5 us -> 5.19 us
  Pallas kernels: 0 us -> 44.2 us
  other arithmetic: 28.3 us -> 0 us
  local copies, waits for them, and re-layouts: 14.4 us -> 4.44 us
    all_gather x2 -> x0, waiting for transfers between devices: 149 us -> none  [the longest x1 77.5 us: per_device(): fragment = lax.all_gather(prompt_pair, 'seq', axis=1, tiled=True)]
    dot_general x4 -> x0, matrix products: 45.5 us -> none  [the longest x2 23.2 us: update_state(): jnp.einsum('rkgn,nkd->rkgd', rounded, value_block, preferred_element_type...]
    pallas_call x0 -> x1, Pallas kernels: none -> 44.2 us  [per_device(): pl.pallas_call(gather_attend, out_shape=jax.ShapeDtypeStruct(queries.shap...]
    reduce_sum x3 -> x0, other arithmetic: 22.5 us -> none  [the longest x2 22.4 us: update_state(): summed = summed * rescale + jnp.sum(weights, axis=3)]
    unnamed x9 -> x2, local copies, waits for them, and re-layouts: 13.6 us -> 4.44 us
    another operation x4 -> x0, other arithmetic: 3.1 us -> none  [the longest x1 1.54 us: per_device(): response_pair = jnp.stack([response_keys, response_values])]
    unnamed x4 -> x2, waiting for transfers between devices: 44.2 us -> 45.4 us
  transfers between devices with their start and end apart: 3 -> 1, of which waited for: 3 -> 1; matrix products, arithmetic and copies ran while one was open for 5% -> 0% of each run, Pallas kernels for 0% -> 0%
where the time goes in v1:
time: 113 us
  waiting for transfers between devices  45.4 us (40%)
  Pallas kernels  44.2 us (39%)
  between operations  13.4 us (12%)
  matrix products  5.19 us (5%)
  local copies, waits for them, and re-layouts  4.44 us (4%)
    unnamed x2, waiting for transfers between devices  45.4 us
    pallas_call x1, Pallas kernels, per_device(): pl.pallas_call(gather_attend, out_shape=jax.ShapeDtypeStruct(queries.shap...  44.2 us
    dot_general x1, matrix products, per_device(): jnp.dot(attended, out_weight, preferred_element_type=jnp.float32)  5.19 us
    unnamed x2, local copies, waits for them, and re-layouts  4.44 us
  transfers between devices with their start and end apart: 1, of which 1 were waited for; matrix products, arithmetic and copies ran while one was open for 0% of the time, Pallas kernels for 0%

profile of v1, /device:TPU:8, one launch (start us, length us, event | category | flops | bytes accessed | tf_op | source)
XLA Modules:
  0.0 112.6 jit_solution(15087801235414068310)
XLA Ops:
  6.5 0.0 reduce-scatter.4.cloned.1.call-start
  6.5 44.2 %gather_attend.1 = bf16[256,640]{1,0:T(8,128)(2,1)} custom-call(s32[16]{0:T(128)} %lengths_ref.1, bf16[256,640]{1,0:T(8,128)(2,1)} %q_ref.1, bf16[128,128]{1,0:T(8,128)(2,1)} %pk_ref.1, bf16[128,128]{1,0:T(8,128)(2,1)} %pv_ref.1, bf16[256,128]{1,0:T(8,128)(2,1)} %rk_ref.1, bf16[256,128]{1,0:T(8,128)(2,1)} %rv_ref.1), custom_call_target="tpu_custom_call" | custom-call | tf_op jit(solution)/shard_map/gather_attend/pallas_call | solution.py:189
  50.7 5.2 %convolution_convert_fusion = bf16[256,5120]{1,0:T(8,128)(2,1)S(1)} fusion(bf16[256,640]{1,0:T(8,128)(2,1)} %gather_attend.1, bf16[640,5120]{1,0:T(8,128)(2,1)} %param.13), kind=kOutput, calls=%fused_computation | convolution fusion | flops 1679032320 | bytes 9502720 | tf_op jit(solution)/shard_map/dot_general | solution.py:210
  55.9 2.6 %copy.8 = bf16[256,5120]{0,1:T(8,128)(2,1)} copy(bf16[256,5120]{1,0:T(8,128)(2,1)S(1)} %convolution_convert_fusion) | data formatting | bytes 5242880
  58.5 0.0 reduce-scatter.4.cloned.1.call-update
  58.5 45.3 %reduce-scatter.4.cloned.1.call-done = bf16[640,256]{1,0:T(8,128)(2,1)} async-done(((bf16[5120,256]{1,0:T(8,128)(2,1)}), bf16[640,256]{1,0:T(8,128)(2,1)}) %reduce-scatter.4.cloned.1.call-update) | async-done | bytes 327696
  103.9 1.9 %copy.9 = bf16[256,640]{1,0:T(8,128)(2,1)} copy(bf16[256,640]{0,1:T(8,128)(2,1)} %bitcast.5) | data formatting | bytes 655360
Async XLA Ops:
  6.5 97.3 %reduce-scatter.4.cloned.1.call-start = ((), (), s32[]{:S(2)}) async-start(), calls=%async_computation.1 | async-start | bytes 2949120
Sparse Core Ops, SparseCore 0:
  58.6 45.1 reduce-scatter.3

commit v2 on v1

--- a/solution.py
+++ b/solution.py
@@ -18,6 +18,11 @@
 RROWS = 256
 SCALE = HD**-0.5 * 1.4426950408889634
 LOW = -1e30
+XS = 4
+COLS = 640
+RA = 128
+RB = RROWS - RA
+ROLES = [(1, 2), (0, 2), (1, 1), (1, 3), (0, 1), (0, 3), (1, 0), (0, 0)]
 MESH = pl.DeviceIdType.MESH
 
 
@@ -57,9 +62,11 @@
         )
 
 
-def gather_attend(
-    lengths_ref, q_ref, pk_ref, pv_ref, rk_ref, rv_ref, out_ref,
-    pbuf, rbuf, top_ref, acc_ref, bias_ref, first_ref, load_sem, send_sem, recv_sem,
+def attention_block(
+    lengths_ref, q_ref, pk_ref, pv_ref, rk_ref, rv_ref, w_ref, out_ref,
+    pbuf, rbuf, top_ref, acc_ref, bias_ref, first_ref, wbuf, att_ref, part,
+    from_y, from_y_late, step1, step2, late1, late2,
+    load_sem, send_sem, recv_sem, psend_sem, precv_sem,
 ):
     s = lax.axis_index("seq")
     z, b = s // 4, s % 4
@@ -68,17 +75,28 @@
     across = {"seq": z * 4 + (1 - h) * 2 + c}
     up = {"seq": ((z + 1) % PLANES) * 4 + b}
     down = {"seq": ((z + PLANES - 1) % PLANES) * 4 + b}
+    t = lax.axis_index("tp")
+    yl, x = t // XS, t % XS
+    right = {"tp": yl * XS + (x + 1) % XS}
+    left = {"tp": yl * XS + (x + XS - 1) % XS}
+    beside = {"tp": (1 - yl) * XS + x}
     order = [h * 2 + c, (1 - h) * 2 + c, h * 2 + (1 - c), (1 - h) * 2 + (1 - c)]
 
     loads = []
     for n, (src, dst) in enumerate(
-        [(pk_ref, pbuf.at[s, 0]), (pv_ref, pbuf.at[s, 1]), (rk_ref, rbuf.at[s, 0]), (rv_ref, rbuf.at[s, 1])]
+        [
+            (pk_ref, pbuf.at[s, 0]),
+            (pv_ref, pbuf.at[s, 1]),
+            (rk_ref, rbuf.at[s, 0]),
+            (rv_ref, rbuf.at[s, 1]),
+            (w_ref, wbuf),
+        ]
     ):
         loads.append(pltpu.make_async_copy(src, dst, load_sem.at[n]))
         loads[-1].start()
 
     barrier = pltpu.get_barrier_semaphore()
-    for peer in (sibling, across, up, down):
+    for peer in (sibling, across, up, down, right, left, beside):
         pl.semaphore_signal(barrier, inc=1, device_id=peer, device_id_type=MESH)
 
     def slot_of(kind, away, which):
@@ -129,9 +147,9 @@
             if shard[2] < 2:
                 pass_on(*shard)
 
-    for copying in loads:
+    for copying in loads[:4]:
         copying.wait()
-    pl.semaphore_wait(barrier, 4)
+    pl.semaphore_wait(barrier, 7)
     pass_on(0, 0, 0)
     pass_on(1, 0, 0)
 
@@ -178,7 +196,94 @@
 
     for head in range(GROUP):
         acc = acc_ref[head]
-        out_ref[:, head * HD : (head + 1) * HD] = (acc[:, :HD] / acc[:, HD:]).astype(jnp.bfloat16)
+        att_ref[:, head * HD : (head + 1) * HD] = (acc[:, :HD] / acc[:, HD:]).astype(jnp.bfloat16)
+
+    loads[4].wait()
+    count = 0
+
+    def hand(src, dst, peer):
+        nonlocal count
+        sending = pltpu.make_async_remote_copy(
+            src_ref=src,
+            dst_ref=dst,
+            send_sem=psend_sem.at[count],
+            recv_sem=precv_sem.at[count],
+            device_id=peer,
+            device_id_type=MESH,
+        )
+        count += 1
+        sending.start()
+        sends.append(sending)
+        return sending
+
+    def compute(role):
+        other, dx = ROLES[role]
+        target = ((1 - yl) if other else yl) * XS + (x + dx) % XS
+        columns = pl.ds(pl.multiple_of(target * COLS, HD), COLS)
+        part[role] = jnp.dot(att_ref[...], wbuf[:, columns], preferred_element_type=jnp.float32).astype(jnp.bfloat16)
+
+    def add(role, rows, *others):
+        total = part[role, rows].astype(jnp.float32)
+        for other in others:
+            total = total + other.astype(jnp.float32)
+        part[role, rows] = total.astype(jnp.bfloat16)
+
+    rows_a, rows_b = slice(0, RA), slice(RA, RROWS)
+    high_a, low_a = slice(0, RA // 2), slice(RA // 2, RA)
+    high_b, low_b = slice(RA, RA + RB // 2), slice(RA + RB // 2, RROWS)
+    ya, b1, b2 = {}, {}, {}
+    compute(0)
+    ya[0] = hand(part.at[0, rows_a], from_y.at[0], beside)
+    b1[0, 0] = hand(part.at[0, high_b], step1.at[0, 0], right)
+    b1[1, 0] = hand(part.at[0, low_b], step1.at[1, 0], left)
+    compute(1)
+    b1[0, 1] = hand(part.at[1, high_b], step1.at[0, 1], right)
+    b1[1, 1] = hand(part.at[1, low_b], step1.at[1, 1], left)
+    compute(2)
+    ya[1] = hand(part.at[2, rows_a], from_y.at[1], beside)
+    compute(3)
+    ya[2] = hand(part.at[3, rows_a], from_y.at[2], beside)
+    compute(6)
+    ya[3] = hand(part.at[6, rows_a], from_y.at[3], beside)
+    compute(4)
+    compute(5)
+    ya[0].wait_recv()
+    add(1, rows_a, from_y[0])
+    a1 = [hand(part.at[1, high_a], late1.at[0], right), hand(part.at[1, low_a], late1.at[1], left)]
+    for n, (to_right, to_left) in enumerate([(2, 3), (4, 5)]):
+        b1[0, n].wait_recv()
+        add(to_right, high_b, step1[0, n])
+        b2[0, n] = hand(part.at[to_right, rows_b], step2.at[0, n], right)
+        b1[1, n].wait_recv()
+        add(to_left, low_b, step1[1, n])
+        b2[1, n] = hand(part.at[to_left, rows_b], step2.at[1, n], left)
+    compute(7)
+    a2 = []
+    for n in range(2):
+        ya[1 + n].wait_recv()
+        add(4 + n, rows_a, from_y[1 + n])
+        a1[n].wait_recv()
+        add(4 + n, low_a if n else high_a, late1[n])
+        a2.append(hand(part.at[4 + n, rows_a], late2.at[n], left if n else right))
+    for n in range(2):
+        b2[n, 0].wait_recv()
+    add(6, rows_b, step2[0, 0], step2[1, 0])
+    yb = hand(part.at[6, rows_b], from_y_late, beside)
+    ya[3].wait_recv()
+    for n in range(2):
+        a2[n].wait_recv()
+
+    def total(rows, *others):
+        result = part[7, rows].astype(jnp.float32)
+        for other in others:
+            result = result + other.astype(jnp.float32)
+        out_ref[rows, :] = result.astype(jnp.bfloat16)
+
+    total(rows_a, from_y[3], late2[0], late2[1])
+    for n in range(2):
+        b2[n, 1].wait_recv()
+    yb.wait_recv()
+    total(rows_b, step2[0, 1], step2[1, 1], from_y_late[...])
 
     for sending in sends:
         sending.wait_send()
@@ -186,10 +291,10 @@
 
 def per_device(queries, prompt_keys, prompt_values, response_keys, response_values, lengths, out_weight):
     vmem = pl.BlockSpec(memory_space=pltpu.VMEM)
-    attended = pl.pallas_call(
-        gather_attend,
-        out_shape=jax.ShapeDtypeStruct(queries.shape, jnp.bfloat16),
-        in_specs=[pl.BlockSpec(memory_space=pltpu.SMEM), vmem] + [pl.BlockSpec(memory_space=pl.ANY)] * 4,
+    return pl.pallas_call(
+        attention_block,
+        out_shape=jax.ShapeDtypeStruct((RROWS, COLS), jnp.bfloat16),
+        in_specs=[pl.BlockSpec(memory_space=pltpu.SMEM), vmem] + [pl.BlockSpec(memory_space=pl.ANY)] * 5,
         out_specs=vmem,
         scratch_shapes=[
             pltpu.VMEM((SLOTS, 2, PROWS, HD), jnp.bfloat16),
@@ -198,17 +303,26 @@
             pltpu.VMEM((GROUP, RROWS, 2 * HD), jnp.float32),
             pltpu.VMEM((RROWS, 5 * RROWS), jnp.float32),
             pltpu.VMEM((RROWS, 1), jnp.int32),
-            pltpu.SemaphoreType.DMA((4,)),
+            pltpu.VMEM(out_weight.shape, jnp.bfloat16),
+            pltpu.VMEM((RROWS, GROUP * HD), jnp.bfloat16),
+            pltpu.VMEM((8, RROWS, COLS), jnp.bfloat16),
+            pltpu.VMEM((4, RA, COLS), jnp.bfloat16),
+            pltpu.VMEM((RB, COLS), jnp.bfloat16),
+            pltpu.VMEM((2, 2, RB // 2, COLS), jnp.bfloat16),
+            pltpu.VMEM((2, 2, RB, COLS), jnp.bfloat16),
+            pltpu.VMEM((2, RA // 2, COLS), jnp.bfloat16),
+            pltpu.VMEM((2, RA, COLS), jnp.bfloat16),
+            pltpu.SemaphoreType.DMA((5,)),
             pltpu.SemaphoreType.DMA((2, 4, SLOTS)),
             pltpu.SemaphoreType.DMA((2, SLOTS)),
+            pltpu.SemaphoreType.DMA((17,)),
+            pltpu.SemaphoreType.DMA((17,)),
         ],
         compiler_params=pltpu.CompilerParams(
             collective_id=0, has_side_effects=True, vmem_limit_bytes=60 * 2**20
         ),
-        name="gather_attend",
-    )(lengths, queries, prompt_keys, prompt_values, response_keys, response_values)
-    partial_out = jnp.dot(attended, out_weight, preferred_element_type=jnp.float32)
-    return lax.psum_scatter(partial_out.astype(jnp.bfloat16), "tp", scatter_dimension=1, tiled=True)
+        name="attention_block",
+    )(lengths, queries, prompt_keys, prompt_values, response_keys, response_values, out_weight)
 
 
 def solution(mesh):

time: 113 us -> 70.7 us (0.63)
  waiting for transfers between devices: 45.4 us -> 0 us
  Pallas kernels: 44.2 us -> 68.5 us
  between operations: 13.4 us -> 0.01 us
  matrix products: 5.19 us -> 0 us
  local copies, waits for them, and re-layouts: 4.44 us -> 1.73 us
    unnamed x2 -> x0, waiting for transfers between devices: 45.4 us -> none
    pallas_call x1, Pallas kernels: 44.2 us -> 68.5 us  [per_device(): pl.pallas_call(attention_block, out_shape=jax.ShapeDtypeStruct((RROWS, CO...]
    dot_general x1 -> x0, matrix products: 5.19 us -> none  [per_device(): jnp.dot(attended, out_weight, preferred_element_type=jnp.float32)]
    unnamed x2 -> x1, local copies, waits for them, and re-layouts: 4.44 us -> 1.73 us
  transfers between devices with their start and end apart: 1 -> 0, of which waited for: 1 -> 0; matrix products, arithmetic and copies ran while one was open for 0% -> 0% of each run, Pallas kernels for 0% -> 0%
where the time goes in v2:
time: 70.7 us; the launch traced here: 70.3 us
  Pallas kernels  68.5 us (97%)
  local copies, waits for them, and re-layouts  1.73 us (2%)
    pallas_call x1, Pallas kernels, per_device(): pl.pallas_call(attention_block, out_shape=jax.ShapeDtypeStruct((RROWS, CO...  68.5 us
    unnamed x1, local copies, waits for them, and re-layouts  1.73 us

profile of v2, /device:TPU:8, one launch (start us, length us, event | category | flops | bytes accessed | tf_op | source)
XLA Modules:
  0.0 70.3 jit_solution(6305056818050858450)
XLA Ops:
  0.0 68.5 %attention_block.1 = bf16[256,640]{1,0:T(8,128)(2,1)} custom-call(s32[16]{0:T(128)} %lengths_ref.1, bf16[256,640]{1,0:T(8,128)(2,1)} %q_ref.1, bf16[128,128]{1,0:T(8,128)(2,1)} %pk_ref.1, bf16[128,128]{1,0:T(8,128)(2,1)} %pv_ref.1, bf16[256,128]{1,0:T(8,128)(2,1)} %rk_ref.1, bf16[256,128]{1,0:T(8,128)(2,1)} %rv_ref.1, bf16[640,5120]{1,0:T(8,128)(2,1)} %w_ref.1), custom_call_target="tpu_custom_call" | custom-call | tf_op jit(solution)/shard_map/attention_block/pallas_call | solution.py:294
  68.5 1.7 %copy.9 = bf16[256,640]{1,0:T(8,128)(2,1)} copy(bf16[256,640]{1,0:T(8,128)(2,1)} %attention_block.1) | data formatting | bytes 655360

commit v3 on v2

v3 whole, which is shorter than its diff:
```python
import functools

import jax
import jax.numpy as jnp
from jax import lax
from jax.experimental import pallas as pl
from jax.experimental.pallas import tpu as pltpu
from jax.sharding import PartitionSpec as P

HEADS = 40
KVH = 8
HD = 128
GROUP = HEADS // KVH
N_RESP = 16
PLANES = 8
SLOTS = 32
PROWS = 128
RROWS = 256
SCALE = HD**-0.5 * 1.4426950408889634
LOW = -1e30
XS = 4
SENDS = 32
ARRIVALS = 78
COLS = 640
RA = 112
RB = RROWS - RA
HA, HB = 64, 80
ROLES = [(1, 2), (0, 2), (1, 1), (1, 3), (0, 1), (0, 3), (1, 0), (0, 0)]
MESH = pl.DeviceIdType.MESH


PLAN = [
    ([(0, 1, 0, 0), (0, -1, 0, 0)], 0, [(0, 2), (1, 0), (-1, 0)], [[]]),
    ([(0, 0, 1, 0), (1, 1, 0, 0), (1, 1, 0, 1), (0, 2, 0, 0), (0, -2, 0, 0)], 0, [(0, 1), (1, 2), (-1, 2), (0, 3), (2, 0), (-2, 0), (2, 2), (-2, 2)], [[(0, -1, 1, 0), (1, 1, 1, 0)]]),
    ([(1, 2, 0, 0), (1, 1, 1, 1), (0, 2, 1, 0), (0, 1, 1, 0), (1, 2, 0, 1)], 1, [(1, 0), (1, 2), (1, 1), (2, 0)], [[(0, 3, 0, 0)]]),
    ([(0, -2, 1, 0)], 0, [(-1, 1), (-1, 3), (2, 1), (1, 1), (2, 3), (1, 3), (3, 0), (-2, 1)], [[(1, 3, 0, 0)]]),
    ([(1, 2, 1, 0), (1, 3, 0, 1), (1, 2, 1, 1)], 1, [(1, 3), (2, 2), (3, 0), (2, 1)], [[(0, 4, 1, 0), (0, 3, 1, 0)]]),
    ([(1, 4, 0, 0), (0, 4, 0, 0), (1, 3, 1, 0), (1, 4, 0, 1)], 0, [(3, 2), (-2, 3), (4, 1), (3, 1), (4, 3), (3, 3), (4, 0), (4, 2)], [[(1, 3, 1, 1)]]),
    ([(0, 5, 1, 0)], 1, [(3, 2), (2, 3), (3, 1), (3, 3)], [[(0, 5, 0, 0)]]),
    ([(1, 4, 1, 0)], 0, [(5, 1), (5, 0), (5, 3), (5, 2)], [[]]),
    ([(1, 4, 1, 1)], 2, [], [[]]),
]

SPLIT = (2, 5)
DOWN, UP = 5, 2


def attend(q_ref, keys, values, bias_ref, top_ref, acc_ref, heads):
    count = keys.shape[0]
    widened = jnp.concatenate([values, jnp.ones((count, HD), jnp.bfloat16)], axis=1)
    for head in heads:
        scores = lax.dot_general(
            q_ref[:, head * HD : (head + 1) * HD],
            keys,
            (((1,), (1,)), ((), ())),
            preferred_element_type=jnp.float32,
        )
        if bias_ref is not None:
            scores = scores + bias_ref[:, :count]
        before = top_ref[head]
        top = jnp.maximum(before, jnp.max(scores, axis=1, keepdims=True) * SCALE)
        weights = jnp.exp2(scores * SCALE - top).astype(jnp.bfloat16)
        top_ref[head] = top
        acc_ref[head] = acc_ref[head] * jnp.exp2(before - top) + jnp.dot(
            weights, widened, preferred_element_type=jnp.float32
        )


def attention_block(
    lengths_hbm, q_hbm, pk_ref, pv_ref, rk_ref, rv_ref, w_ref, out_hbm,
    pbuf, rbuf, top_ref, acc_ref, bias_ref, first_ref, wbuf, att_ref, part,
    from_y, from_y_late, step1_r, step1_l, step2, late1_r, late1_l, late2,
    lengths_ref, q_ref, out_ref,
    load_sem, send_sem, recv_sem,
):
    s = lax.axis_index("seq")
    z, b = s // 4, s % 4
    h, c = b // 2, b % 2
    sibling = {"seq": z * 4 + h * 2 + (1 - c)}
    across = {"seq": z * 4 + (1 - h) * 2 + c}
    up = {"seq": ((z + 1) % PLANES) * 4 + b}
    up_two = {"seq": ((z + 2) % PLANES) * 4 + b}
    down_two = {"seq": ((z + PLANES - 2) % PLANES) * 4 + b}
    down = {"seq": ((z + PLANES - 1) % PLANES) * 4 + b}
    t = lax.axis_index("tp")
    yl, x = t // XS, t % XS
    right = {"tp": yl * XS + (x + 1) % XS}
    left = {"tp": yl * XS + (x + XS - 1) % XS}
    beside = {"tp": (1 - yl) * XS + x}
    order = [h * 2 + c, (1 - h) * 2 + c, h * 2 + (1 - c), (1 - h) * 2 + (1 - c)]

    loads = []
    for n, (src, dst) in enumerate(
        [
            (pk_ref, pbuf.at[s, 0]),
            (pv_ref, pbuf.at[s, 1]),
            (rk_ref, rbuf.at[s, 0]),
            (rv_ref, rbuf.at[s, 1]),
            (lengths_hbm, lengths_ref),
            (q_hbm, q_ref),
            (w_ref, wbuf),
        ]
    ):
        loads.append(pltpu.make_async_copy(src, dst, load_sem.at[n]))
        loads[-1].start()

    barrier = pltpu.get_barrier_semaphore()
    for peer in (sibling, across, up, down, right, left, beside, up_two, down_two):
        pl.semaphore_signal(barrier, inc=1, device_id=peer, device_id_type=MESH)

    def slot_of(kind, away, which):
        plane = (z + (PLANES - away if kind else PLANES + away)) % PLANES
        return plane * 4 + order[which]

    names = {}

    def name_of(*what):
        return names.setdefault(what, len(names))

    sends = []

    def start(src, dst, name, peer, only=None):
        number = len(sends)
        if number >= SENDS:
            finish(sends[number - SENDS])
        sending = pltpu.make_async_remote_copy(
            src_ref=src,
            dst_ref=dst,
            send_sem=send_sem.at[number % SENDS],
            recv_sem=recv_sem.at[name],
            device_id=peer,
            device_id_type=MESH,
        )
        sends.append((sending, only))
        if only is None:
            sending.start()
        else:
            pl.when(only)(sending.start)
        return sending

    def finish(entry):
        sending, only = entry
        if only is None:
            sending.wait_send()
        else:
            pl.when(only)(sending.wait_send)

    def part_of(kind, slot, piece):
        buf = rbuf if kind else pbuf
        return buf.at[slot] if piece == 2 else buf.at[slot, piece]

    def pass_on(kind, away, which, piece):
        slot = slot_of(kind, away, which)
        ref = part_of(kind, slot, piece)
        only = None
        if kind == 0:
            if which == 0:
                if away == 0:
                    start(ref, ref, name_of(0, 0, 1, 2), across)
                if 0 <= away < DOWN:
                    start(ref, ref, name_of(0, away + 1, 0, 2), down)
            elif away >= 0 and away % 2 == 0:
                if away + 2 <= DOWN:
                    start(ref, ref, name_of(0, away + 2, 1, 2), down_two)
                if away + 1 <= DOWN:
                    start(ref, ref, name_of(0, away + 1, 1, 2), down)
            if -UP < away <= 0:
                start(ref, ref, name_of(0, away - 1, which, 2), up)
        elif which == 0:
            if away < 4:
                start(ref, ref, name_of(1, away + 1, 0, piece), up)
            start(ref, ref, name_of(1, away, 1, piece), across, {0: h == 0, 4: h == 1}.get(away))
        else:
            only = {0: h == 1, 4: h == 0}.get(away)
        if piece > 0:
            ref = part_of(kind, slot, 2)
            start(ref, ref, name_of(kind, away, which + 2, 2), sibling, only)

    taken = {(0, 0, 0, 2), (1, 0, 0, 0), (1, 0, 0, 1)}

    def take(kind, away, which, piece):
        piece = piece if kind and which < 2 else 2
        if (kind, away, which, piece) in taken:
            return
        if piece == 1:
            take(kind, away, which, 0)
        taken.add((kind, away, which, piece))
        ref = part_of(kind, slot_of(kind, away, which), piece)
        number = name_of(kind, away, which, piece)
        arriving = pltpu.make_async_remote_copy(
            src_ref=ref,
            dst_ref=ref,
            send_sem=send_sem.at[0],
            recv_sem=recv_sem.at[number],
            device_id=sibling,
            device_id_type=MESH,
        )
        only = {0: h == 1, 4: h == 0}.get(away) if kind and which % 2 else None
        if only is None:
            arriving.wait_recv()
        else:
            pl.when(only)(arriving.wait_recv)
        if which < 2:
            pass_on(kind, away, which, piece)

    def visible(slot, at):
        position = s * RROWS + lax.broadcasted_iota(jnp.int32, (RROWS, 1), 0)
        key = slot * RROWS + lax.broadcasted_iota(jnp.int32, (RROWS, RROWS), 1)
        seen = (key >= first_ref[...]) & (key <= position)
        bias_ref[:, at : at + RROWS] = jnp.where(seen, 0.0, LOW)

    loads[4].wait()
    position = s * RROWS + lax.broadcasted_iota(jnp.int32, (RROWS, 1), 0)
    first = jnp.zeros((RROWS, 1), jnp.int32)
    begin = jnp.int32(0)
    for r in range(N_RESP):
        first = jnp.where(position >= begin, begin, first)
        begin = begin + lengths_ref[r]
    first_ref[...] = first
    top_ref[...] = jnp.full_like(top_ref, LOW)
    acc_ref[...] = jnp.zeros_like(acc_ref)
    for copying in loads[:4]:
        copying.wait()
    pl.semaphore_wait(barrier, 9)
    pass_on(0, 0, 0, 2)
    pass_on(1, 0, 0, 0)
    pass_on(1, 0, 0, 1)
    bias_ref[:, :PROWS] = jnp.zeros((RROWS, PROWS), jnp.float32)
    visible(s, PROWS)
    loads[5].wait()
    keys, values = [jnp.concatenate([pbuf[s, n], rbuf[s, n]], axis=0) for n in range(2)]
    attend(q_ref, keys, values, bias_ref, top_ref, acc_ref, range(GROUP))

    for step, (before, kind, shards, between) in enumerate(PLAN):
        for piece in before:
            take(*piece)
        if step == 1:
            take(1, 0, 1, 0)
            take(1, 0, 1, 1)
        for away, which in shards:
            for piece in range(kind + 1):
                take(kind, away, which, piece)
        if kind < 2:
            chosen = [slot_of(kind, *shard) for shard in shards]
        else:
            for away in (0, 4):
                for which in range(4):
                    take(1, away, which, 0)
                    take(1, away, which, 1)
            near = [slot_of(1, 0, which) for which in range(4)]
            far = [slot_of(1, 4, which) for which in range(4)]
            chosen = [far[0], c * near[2] + (1 - c) * far[2]] + [h * near[n] + (1 - h) * far[n] for n in (1, 3)]
        buf = rbuf if kind else pbuf
        if kind:
            for n, slot in enumerate(chosen):
                visible(slot, n * RROWS)
        keys, values = [jnp.concatenate([buf[slot, n] for slot in chosen], axis=0) for n in range(2)]
        edges = (0,) + SPLIT
        for n in range(len(SPLIT)):
            attend(q_ref, keys, values, bias_ref if kind else None, top_ref, acc_ref, range(edges[n], edges[n + 1]))
            if n < len(between):
                for piece in between[n]:
                    take(*piece)

    for head in range(GROUP):
        acc = acc_ref[head]
        att_ref[:, head * HD : (head + 1) * HD] = (acc[:, :HD] / acc[:, HD:]).astype(jnp.bfloat16)

    loads[6].wait()

    def hand(src, dst, peer):
        return start(src, dst, name_of(len(names)), peer)

    def compute(role):
        other, dx = ROLES[role]
        target = ((1 - yl) if other else yl) * XS + (x + dx) % XS
        columns = pl.ds(pl.multiple_of(target * COLS, HD), COLS)
        part[role] = jnp.dot(att_ref[...], wbuf[:, columns], preferred_element_type=jnp.float32).astype(jnp.bfloat16)

    def add(role, rows, *others):
        total = part[role, rows].astype(jnp.float32)
        for other in others:
            total = total + other.astype(jnp.float32)
        part[role, rows] = total.astype(jnp.bfloat16)

    rows_a, rows_b = slice(0, RA), slice(RA, RROWS)
    high_a, low_a = slice(0, HA), slice(HA, RA)
    high_b, low_b = slice(RA, RA + HB), slice(RA + HB, RROWS)
    ya, b1, b2 = {}, {}, {}
    compute(0)
    ya[0] = hand(part.at[0, rows_a], from_y.at[0], beside)
    b1[0, 0] = hand(part.at[0, high_b], step1_r.at[0], right)
    b1[1, 0] = hand(part.at[0, low_b], step1_l.at[0], left)
    compute(1)
    b1[0, 1] = hand(part.at[1, high_b], step1_r.at[1], right)
    b1[1, 1] = hand(part.at[1, low_b], step1_l.at[1], left)
    compute(2)
    ya[1] = hand(part.at[2, rows_a], from_y.at[1], beside)
    compute(3)
    ya[2] = hand(part.at[3, rows_a], from_y.at[2], beside)
    compute(6)
    ya[3] = hand(part.at[6, rows_a], from_y.at[3], beside)
    compute(4)
    compute(5)
    ya[0].wait_recv()
    add(1, rows_a, from_y[0])
    a1 = [hand(part.at[1, high_a], late1_r, right), hand(part.at[1, low_a], late1_l, left)]
    for n, (to_right, to_left) in enumerate([(2, 3), (4, 5)]):
        b1[0, n].wait_recv()
        add(to_right, high_b, step1_r[n])
        b2[0, n] = hand(part.at[to_right, rows_b], step2.at[0, n], right)
        b1[1, n].wait_recv()
        add(to_left, low_b, step1_l[n])
        b2[1, n] = hand(part.at[to_left, rows_b], step2.at[1, n], left)
    compute(7)
    a2 = []
    for n in range(2):
        ya[1 + n].wait_recv()
        add(4 + n, rows_a, from_y[1 + n])
        a1[n].wait_recv()
        add(4 + n, low_a if n else high_a, (late1_l if n else late1_r)[...])
        a2.append(hand(part.at[4 + n, rows_a], late2.at[n], left if n else right))
    for n in range(2):
        b2[n, 0].wait_recv()
    add(6, rows_b, step2[0, 0], step2[1, 0])
    yb = hand(part.at[6, rows_b], from_y_late, beside)
    ya[3].wait_recv()
    for n in range(2):
        a2[n].wait_recv()

    def total(rows, *others):
        result = part[7, rows].astype(jnp.float32)
        for other in others:
            result = result + other.astype(jnp.float32)
        out_ref[rows, :] = result.astype(jnp.bfloat16)

    total(rows_a, from_y[3], late2[0], late2[1])
    stores = [pltpu.make_async_copy(out_ref.at[rows], out_hbm.at[rows], load_sem.at[n]) for n, rows in enumerate((rows_a, rows_b))]
    stores[0].start()
    for n in range(2):
        b2[n, 1].wait_recv()
    yb.wait_recv()
    total(rows_b, step2[0, 1], step2[1, 1], from_y_late[...])
    stores[1].start()
    for entry in sends[-SENDS:]:
        finish(entry)
    for storing in stores:
        storing.wait()
    assert len(names) <= ARRIVALS


def per_device(queries, prompt_keys, prompt_values, response_keys, response_values, lengths, out_weight):
    anywhere = pl.BlockSpec(memory_space=pl.ANY)
    return pl.pallas_call(
        attention_block,
        out_shape=jax.ShapeDtypeStruct((RROWS, COLS), jnp.bfloat16),
        in_specs=[anywhere] * 7,
        out_specs=anywhere,
        scratch_shapes=[
            pltpu.VMEM((SLOTS, 2, PROWS, HD), jnp.bfloat16),
            pltpu.VMEM((SLOTS, 2, RROWS, HD), jnp.bfloat16),
            pltpu.VMEM((GROUP, RROWS, 1), jnp.float32),
            pltpu.VMEM((GROUP, RROWS, 2 * HD), jnp.float32),
            pltpu.VMEM((RROWS, 4 * RROWS), jnp.float32),
            pltpu.VMEM((RROWS, 1), jnp.int32),
            pltpu.VMEM(out_weight.shape, jnp.bfloat16),
            pltpu.VMEM((RROWS, GROUP * HD), jnp.bfloat16),
            pltpu.VMEM((8, RROWS, COLS), jnp.bfloat16),
            pltpu.VMEM((4, RA, COLS), jnp.bfloat16),
            pltpu.VMEM((RB, COLS), jnp.bfloat16),
            pltpu.VMEM((2, HB, COLS), jnp.bfloat16),
            pltpu.VMEM((2, RB - HB, COLS), jnp.bfloat16),
            pltpu.VMEM((2, 2, RB, COLS), jnp.bfloat16),
            pltpu.VMEM((HA, COLS), jnp.bfloat16),
            pltpu.VMEM((RA - HA, COLS), jnp.bfloat16),
            pltpu.VMEM((2, RA, COLS), jnp.bfloat16),
            pltpu.SMEM((N_RESP,), jnp.int32),
            pltpu.VMEM((RROWS, GROUP * HD), jnp.bfloat16),
            pltpu.VMEM((RROWS, COLS), jnp.bfloat16),
            pltpu.SemaphoreType.DMA((7,)),
            pltpu.SemaphoreType.DMA((SENDS,)),
            pltpu.SemaphoreType.DMA((ARRIVALS,)),
        ],
        compiler_params=pltpu.CompilerParams(
            collective_id=0, has_side_effects=True, vmem_limit_bytes=60 * 2**20
        ),
        name="attention_block",
    )(lengths, queries, prompt_keys, prompt_values, response_keys, response_values, out_weight)


def solution(mesh):
    in_specs = (P("seq", "tp"), P("seq", "tp"), P("seq", "tp"), P("seq", "tp"), P("seq", "tp"), P(), P("tp", None))
    return jax.shard_map(
        per_device, mesh=mesh, in_specs=in_specs, out_specs=P("seq", "tp"), check_vma=False
    )
```

time: 70.7 us -> 66.2 us (0.936)
  Pallas kernels: 68.5 us -> 64.3 us
    pallas_call x1, Pallas kernels: 68.5 us -> 64.3 us  [per_device(): pl.pallas_call(attention_block, out_shape=jax.ShapeDtypeStruct((RROWS, CO...]
where the time goes in v3:
time: 66.2 us; the launch traced here: 66 us
  Pallas kernels  64.3 us (97%)
  local copies, waits for them, and re-layouts  1.73 us (3%)
    pallas_call x1, Pallas kernels, per_device(): pl.pallas_call(attention_block, out_shape=jax.ShapeDtypeStruct((RROWS, CO...  64.3 us
    unnamed x1, local copies, waits for them, and re-layouts  1.73 us

profile of v3, /device:TPU:8, one launch (start us, length us, event | category | flops | bytes accessed | tf_op | source)
XLA Modules:
  0.0 66.0 jit_solution(15266414755011920882)
XLA Ops:
  0.0 64.3 %attention_block.1 = bf16[256,640]{1,0:T(8,128)(2,1)} custom-call(s32[16]{0:T(128)} %lengths_hbm.1, bf16[256,640]{1,0:T(8,128)(2,1)} %q_hbm.1, bf16[128,128]{1,0:T(8,128)(2,1)} %pk_ref.1, bf16[128,128]{1,0:T(8,128)(2,1)} %pv_ref.1, bf16[256,128]{1,0:T(8,128)(2,1)} %rk_ref.1, bf16[256,128]{1,0:T(8,128)(2,1)} %rv_ref.1, bf16[640,5120]{1,0:T(8,128)(2,1)} %w_ref.1), custom_call_target="tpu_custom_call" | custom-call | tf_op jit(solution)/shard_map/attention_block/pallas_call | solution.py:354
  64.3 1.7 %copy.9 = bf16[256,640]{1,0:T(8,128)(2,1)} copy(bf16[256,640]{1,0:T(8,128)(2,1)} %attention_block.1) | data formatting | bytes 655360

commit v4 on v3

--- a/solution.py
+++ b/solution.py
@@ -30,19 +30,17 @@
 
 
 PLAN = [
-    ([(0, 1, 0, 0), (0, -1, 0, 0)], 0, [(0, 2), (1, 0), (-1, 0)], [[]]),
-    ([(0, 0, 1, 0), (1, 1, 0, 0), (1, 1, 0, 1), (0, 2, 0, 0), (0, -2, 0, 0)], 0, [(0, 1), (1, 2), (-1, 2), (0, 3), (2, 0), (-2, 0), (2, 2), (-2, 2)], [[(0, -1, 1, 0), (1, 1, 1, 0)]]),
-    ([(1, 2, 0, 0), (1, 1, 1, 1), (0, 2, 1, 0), (0, 1, 1, 0), (1, 2, 0, 1)], 1, [(1, 0), (1, 2), (1, 1), (2, 0)], [[(0, 3, 0, 0)]]),
-    ([(0, -2, 1, 0)], 0, [(-1, 1), (-1, 3), (2, 1), (1, 1), (2, 3), (1, 3), (3, 0), (-2, 1)], [[(1, 3, 0, 0)]]),
-    ([(1, 2, 1, 0), (1, 3, 0, 1), (1, 2, 1, 1)], 1, [(1, 3), (2, 2), (3, 0), (2, 1)], [[(0, 4, 1, 0), (0, 3, 1, 0)]]),
-    ([(1, 4, 0, 0), (0, 4, 0, 0), (1, 3, 1, 0), (1, 4, 0, 1)], 0, [(3, 2), (-2, 3), (4, 1), (3, 1), (4, 3), (3, 3), (4, 0), (4, 2)], [[(1, 3, 1, 1)]]),
-    ([(0, 5, 1, 0)], 1, [(3, 2), (2, 3), (3, 1), (3, 3)], [[(0, 5, 0, 0)]]),
-    ([(1, 4, 1, 0)], 0, [(5, 1), (5, 0), (5, 3), (5, 2)], [[]]),
-    ([(1, 4, 1, 1)], 2, [], [[]]),
+    ([(1, 1, 0, 0), (0, 1, 0, 0), (0, 0, 1, 0), (1, 1, 0, 1), (0, -1, 0, 0), (0, 2, 0, 0)], 0, [(0, 2), (1, 0), (0, 1), (1, 2), (0, 3), (-1, 0), (2, 0), (-1, 2)], []),
+    ([(1, 2, 0, 0), (1, 1, 1, 0), (0, -1, 1, 0), (1, 1, 1, 1), (1, 2, 0, 1)], 1, [(1, 0), (1, 2), (1, 1), (2, 0)], []),
+    ([(0, 2, 1, 0), (0, 1, 1, 0), (0, -2, 0, 0), (0, 3, 0, 0), (1, 3, 0, 0)], 0, [(2, 2), (-1, 1), (-1, 3), (2, 1), (1, 1), (-2, 0), (3, 0), (2, 3)], []),
+    ([(1, 2, 1, 0), (0, -2, 1, 0), (1, 2, 1, 1), (1, 3, 0, 1)], 1, [(1, 3), (2, 2), (2, 1), (3, 0)], []),
+    ([(0, -3, 0, 0), (1, 3, 1, 0), (0, 4, 1, 0), (0, 3, 1, 0)], 0, [(1, 3), (-2, 2), (3, 2), (-2, 1), (-2, 3), (-3, 0), (4, 1), (3, 1)], []),
+    ([(1, 4, 0, 0), (0, 4, 0, 0), (0, -3, 1, 0), (1, 3, 1, 1), (1, 4, 0, 1)], 0, [(-3, 2), (4, 3), (3, 3), (4, 0), (-3, 1), (4, 2), (-3, 3)], []),
+    ([], 1, [(2, 3), (3, 2), (3, 1), (3, 3)], []),
+    ([(1, 4, 1, 0), (1, 4, 1, 1)], 2, [], []),
 ]
-
-SPLIT = (2, 5)
-DOWN, UP = 5, 2
+SPLIT = (5,)
+DOWN, UP = 4, 3
 
 
 def attend(q_ref, keys, values, bias_ref, top_ref, acc_ref, heads):

time: 66.2 us -> 64.7 us (0.977)
  Pallas kernels: 64.3 us -> 62.9 us
    pallas_call x1, Pallas kernels: 64.3 us -> 62.9 us  [per_device(): pl.pallas_call(attention_block, out_shape=jax.ShapeDtypeStruct((RROWS, CO...]
where the time goes in v4:
time: 64.7 us; the launch traced here: 64.6 us
  Pallas kernels  62.9 us (97%)
  local copies, waits for them, and re-layouts  1.73 us (3%)
    pallas_call x1, Pallas kernels, per_device(): pl.pallas_call(attention_block, out_shape=jax.ShapeDtypeStruct((RROWS, CO...  62.9 us
    unnamed x1, local copies, waits for them, and re-layouts  1.73 us

profile of v4, /device:TPU:8, one launch (start us, length us, event | category | flops | bytes accessed | tf_op | source)
XLA Modules:
  0.0 64.6 jit_solution(10502723947910160936)
XLA Ops:
  0.0 62.9 %attention_block.1 = bf16[256,640]{1,0:T(8,128)(2,1)} custom-call(s32[16]{0:T(128)} %lengths_hbm.1, bf16[256,640]{1,0:T(8,128)(2,1)} %q_hbm.1, bf16[128,128]{1,0:T(8,128)(2,1)} %pk_ref.1, bf16[128,128]{1,0:T(8,128)(2,1)} %pv_ref.1, bf16[256,128]{1,0:T(8,128)(2,1)} %rk_ref.1, bf16[256,128]{1,0:T(8,128)(2,1)} %rv_ref.1, bf16[640,5120]{1,0:T(8,128)(2,1)} %w_ref.1), custom_call_target="tpu_custom_call" | custom-call | tf_op jit(solution)/shard_map/attention_block/pallas_call | solution.py:352
  62.9 1.7 %copy.9 = bf16[256,640]{1,0:T(8,128)(2,1)} copy(bf16[256,640]{1,0:T(8,128)(2,1)} %attention_block.1) | data formatting | bytes 655360

commit v5 on v4

--- a/solution.py
+++ b/solution.py
@@ -300,10 +300,12 @@
     ya[3] = hand(part.at[6, rows_a], from_y.at[3], beside)
     compute(4)
     compute(5)
-    ya[0].wait_recv()
-    add(1, rows_a, from_y[0])
-    a1 = [hand(part.at[1, high_a], late1_r, right), hand(part.at[1, low_a], late1_l, left)]
+    a1 = []
     for n, (to_right, to_left) in enumerate([(2, 3), (4, 5)]):
+        if n:
+            ya[0].wait_recv()
+            add(1, rows_a, from_y[0])
+            a1 += [hand(part.at[1, high_a], late1_r, right), hand(part.at[1, low_a], late1_l, left)]
         b1[0, n].wait_recv()
         add(to_right, high_b, step1_r[n])
         b2[0, n] = hand(part.at[to_right, rows_b], step2.at[0, n], right)

time: 64.7 us -> 64.8 us (level)
  no operation moved by 1% of the time
where the time goes in v5:
time: 64.8 us; the launch traced here: 64.4 us
  Pallas kernels  62.7 us (97%)
  local copies, waits for them, and re-layouts  1.73 us (3%)
    pallas_call x1, Pallas kernels, per_device(): pl.pallas_call(attention_block, out_shape=jax.ShapeDtypeStruct((RROWS, CO...  62.7 us
    unnamed x1, local copies, waits for them, and re-layouts  1.73 us

profile of v5, /device:TPU:8, one launch (start us, length us, event | category | flops | bytes accessed | tf_op | source)
XLA Modules:
  0.0 64.4 jit_solution(9048273460021156807)
XLA Ops:
  0.0 62.7 %attention_block.1 = bf16[256,640]{1,0:T(8,128)(2,1)} custom-call(s32[16]{0:T(128)} %lengths_hbm.1, bf16[256,640]{1,0:T(8,128)(2,1)} %q_hbm.1, bf16[128,128]{1,0:T(8,128)(2,1)} %pk_ref.1, bf16[128,128]{1,0:T(8,128)(2,1)} %pv_ref.1, bf16[256,128]{1,0:T(8,128)(2,1)} %rk_ref.1, bf16[256,128]{1,0:T(8,128)(2,1)} %rv_ref.1, bf16[640,5120]{1,0:T(8,128)(2,1)} %w_ref.1), custom_call_target="tpu_custom_call" | custom-call | tf_op jit(solution)/shard_map/attention_block/pallas_call | solution.py:354
  62.7 1.7 %copy.9 = bf16[256,640]{1,0:T(8,128)(2,1)} copy(bf16[256,640]{1,0:T(8,128)(2,1)} %attention_block.1) | data formatting | bytes 655360
